TPU v7x, 32 devices: a whole 2x2x4 slice. The times are simulated.
32 devices in a mesh: groups: 2 (over y), seq: 4 (over z), mp: 4 (over x, core).
Axes of the slice: x: 2, y: 2, z: 4, core: 2. Of those that a mesh axis runs over, the one named last changes fastest.
Arguments:
- node_vectors: bfloat16 [1024, 2048], P(('groups', 'seq'), 'mp'), parts along dimension 0, may hold values from -6 to 6
- standardize_multiplier: float32 [2048], replicated, may hold values from 0.1 to 1.9
- probe_matrix: bfloat16 [2048, 1024], P(None, 'mp'), may hold values from -1 to 1
- lookup_matrix: bfloat16 [2048, 1024], P(None, 'mp'), may hold values from -1 to 1
- content_matrix: bfloat16 [2048, 1024], P(None, 'mp'), may hold values from -0.125 to 0.125
- softness_per_group: float32 [8], P('mp'), may hold values from 0.5 to 12
- exit_matrix: bfloat16 [1024, 2048], P('mp'), may hold values from -0.1875 to 0.1875
Outputs:
- mixed: bfloat16 [1024, 2048], P(('groups', 'seq'), 'mp'), parts along dimension 0
There are 2 independent parts, one for each index of `groups`. A program takes and returns all parts, laid end to end along the dimension named above; an argument that names none is the same for every part. Nothing has to cross between parts.
All inputs are finite; a program needn't handle non-finite values.
Results may differ from a plain program's by a relative error of at most 0.011.
Values may be sent and summed in bfloat16 or wider, within the bound.
A program may use at most 64 MiB of HBM per device.

v0:
```python
import math
import jax
import jax.numpy as jnp
from jax import lax
from jax.sharding import PartitionSpec as P


def attend(state_in, blocks, query_heads, inverse_root_span, resident_groups, channel_span):
    running_max, running_sum, weighted = state_in
    key_block, value_block = blocks
    count = key_block.shape[0]
    key_heads = key_block.reshape(count, resident_groups, channel_span)
    value_heads = value_block.reshape(count, resident_groups, channel_span)
    scores = (
        jnp.einsum("rhd,nhd->hrn", query_heads, key_heads, preferred_element_type=jnp.float32)
        * inverse_root_span[:, None, None]
    )
    new_max = jnp.max(scores, axis=-1)
    rescale = jnp.exp(running_max - new_max)
    weights = jnp.exp(scores - new_max[:, :, None])
    running_sum = running_sum * rescale + jnp.sum(weights, axis=-1)
    update = jnp.einsum(
        "hrn,nhd->hrd",
        weights.astype(jnp.bfloat16),
        value_heads,
        preferred_element_type=jnp.float32,
    )
    weighted = weighted * rescale[:, :, None] + update
    return (new_max, running_sum, weighted)


def per_device(
    node_vectors,
    standardize_multiplier,
    probe_matrix,
    lookup_matrix,
    content_matrix,
    softness_per_group,
    exit_matrix,
):
    full_rows = lax.all_gather(node_vectors, "mp", axis=1, tiled=True)
    widened = full_rows.astype(jnp.float32)
    average = jnp.mean(widened, axis=-1, keepdims=True)
    centered = widened - average
    variance = jnp.mean(centered * centered, axis=-1, keepdims=True)
    normed = (centered * lax.rsqrt(variance + 1e-05) * standardize_multiplier).astype(jnp.bfloat16)
    queries = jnp.dot(normed, probe_matrix, preferred_element_type=jnp.float32).astype(jnp.bfloat16)
    key_rows = jnp.dot(normed, lookup_matrix, preferred_element_type=jnp.float32).astype(
        jnp.bfloat16
    )
    value_rows = jnp.dot(normed, content_matrix, preferred_element_type=jnp.float32).astype(
        jnp.bfloat16
    )
    resident_groups = softness_per_group.shape[0]
    head_cols = queries.shape[1]
    channel_span = head_cols // resident_groups
    token_count = queries.shape[0]
    query_heads = queries.reshape(token_count, resident_groups, channel_span)
    inverse_root_span = softness_per_group / math.sqrt(channel_span)
    initial = (
        jnp.full((resident_groups, token_count), -jnp.inf, jnp.float32),
        jnp.zeros((resident_groups, token_count), jnp.float32),
        jnp.zeros((resident_groups, token_count, channel_span), jnp.float32),
    )
    final = attend(
        initial,
        (
            lax.all_gather(key_rows, "seq", axis=0, tiled=True),
            lax.all_gather(value_rows, "seq", axis=0, tiled=True),
        ),
        query_heads,
        inverse_root_span,
        resident_groups,
        channel_span,
    )
    heads_out = (
        (final[2] / final[1][:, :, None])
        .transpose(1, 0, 2)
        .reshape(token_count, head_cols)
        .astype(jnp.bfloat16)
    )
    partial_sums = jnp.dot(heads_out, exit_matrix, preferred_element_type=jnp.float32)
    summed = lax.psum_scatter(
        partial_sums.astype(jnp.bfloat16), "mp", scatter_dimension=1, tiled=True
    ).astype(jnp.float32)
    return (node_vectors.astype(jnp.float32) + summed).astype(jnp.bfloat16)


def solution(mesh):
    return jax.shard_map(
        per_device,
        mesh=mesh,
        in_specs=(
            P(("groups", "seq"), "mp"),
            P(),
            P(None, "mp"),
            P(None, "mp"),
            P(None, "mp"),
            P("mp"),
            P("mp", None),
        ),
        out_specs=P(("groups", "seq"), "mp"),
        check_vma=False,
    )
```

profile of v0, /device:TPU:0, one launch (start us, length us, event | category | flops | bytes accessed | tf_op | source)
XLA Modules:
  0.0 81.6 jit_solution(14585379958456140718)
XLA Ops:
  6.5 0.0 copy-start
  6.5 0.0 copy-start.2
  6.5 0.0 reduce-scatter.2.cloned.1.call-start
  6.5 0.8 broadcast_multiply_fusion
  7.3 8.8 %all_gather.9 = bf16[128,2048]{1,0:T(8,128)(2,1)S(1)} all-gather(bf16[128,512]{1,0:T(8,128)(2,1)} %param.7), channel_id=1, replica_groups=mesh['groups'=2,'seq'=4,'mp'=4] {'mp'}, dimensions={1}, use_global_device_ids=true | all-gather | bytes 655360 | tf_op jit(solution)/shard_map/all_gather | solution.py:41
  16.2 0.2 convert_reduce_fusion
  16.4 0.0 copy-start.5
  16.4 0.3 fusion.6
  16.7 0.0 copy-done.2
  16.7 0.4 copy-done.5
  17.1 0.0 copy-start.3
  17.1 0.4 convolution_convert_fusion.2
  17.4 0.9 %copy-done.3 = bf16[2048,256]{1,0:T(8,128)(2,1)S(1)} copy-done((bf16[2048,256]{1,0:T(8,128)(2,1)S(1)}, bf16[2048,256]{1,0:T(8,128)(2,1)}, u32[]{:S(2)}) %copy-start.3) | copy-done | bytes 1048600
  18.3 0.0 copy-start.4
  18.3 0.4 convolution_convert_fusion.1
  18.6 0.9 %copy-done.4 = bf16[2048,256]{1,0:T(8,128)(2,1)S(1)} copy-done((bf16[2048,256]{1,0:T(8,128)(2,1)S(1)}, bf16[2048,256]{1,0:T(8,128)(2,1)}, u32[]{:S(2)}) %copy-start.4) | copy-done | bytes 1048600
  19.5 0.4 fusion.5
  19.9 14.1 %all_gather.11 = bf16[512,256]{1,0:T(8,128)(2,1)S(1)} all-gather(bf16[128,256]{1,0:T(8,128)(2,1)S(1)} %convolution_convert_fusion.1), channel_id=1, replica_groups=mesh['groups'=2,'seq'=4,'mp'=4] {'seq'}, dimensions={0}, use_global_device_ids=true | all-gather | bytes 327680 | tf_op jit(solution)/shard_map/all_gather | solution.py:69
  34.0 0.1 copy.11
  34.1 14.6 %all_gather.10 = bf16[512,256]{1,0:T(8,128)(2,1)S(1)} all-gather(bf16[128,256]{1,0:T(8,128)(2,1)S(1)} %convolution_convert_fusion.2), channel_id=1, replica_groups=mesh['groups'=2,'seq'=4,'mp'=4] {'seq'}, dimensions={0}, use_global_device_ids=true | all-gather | bytes 327680 | tf_op jit(solution)/shard_map/all_gather | solution.py:68
  48.7 0.3 fusion.20
  49.1 0.2 fusion.9
  49.3 0.3 fusion.4
  49.6 0.0 copy-done
  49.6 1.1 %convolution_convert_fusion = bf16[128,2048]{1,0:T(8,128)(2,1)} fusion(bf16[128,256]{0,1:T(8,128)(2,1)S(1)} %bitcast.39, bf16[256,2048]{1,0:T(8,128)(2,1)S(1)} %copy-done), kind=kOutput, calls=%fused_computation | convolution fusion | flops 134479872 | bytes 1638400 | tf_op jit(solution)/shard_map/dot_general | solution.py:82
  50.8 0.0 copy-start.1
  50.8 0.0 reduce-scatter.2.cloned.1.call-update
  50.8 22.4 %reduce-scatter.2.cloned.1.call-done = bf16[128,512]{1,0:T(8,128)(2,1)} async-done(((bf16[128,2048]{1,0:T(8,128)(2,1)}), bf16[128,512]{1,0:T(8,128)(2,1)}) %reduce-scatter.2.cloned.1.call-update) | async-done | bytes 131088 | tf_op jit(solution)/shard_map/reduce_scatter | solution.py:83
  73.2 0.0 copy-done.1
  73.2 1.6 %add_convert_fusion = bf16[128,512]{1,0:T(8,128)(2,1)} fusion(bf16[128,512]{1,0:T(8,128)(2,1)} %reduce-scatter.2.cloned.1.call-done, bf16[128,512]{1,0:T(8,128)(2,1)S(1)} %copy-done.1), kind=kLoop, calls=%fused_computation.22 | loop fusion | flops 262144 | bytes 393216 | tf_op jit(solution)/shard_map/convert_element_type | solution.py:86
  (4 shorter events, 0.0 us)
Async XLA Ops:
  6.5 43.1 %copy-start = (bf16[256,2048]{1,0:T(8,128)(2,1)S(1)}, bf16[256,2048]{1,0:T(8,128)(2,1)}, u32[]{:S(2)}) copy-start(bf16[256,2048]{1,0:T(8,128)(2,1)} %param.13) | copy-start | bytes 3145732
  6.5 10.1 %copy-start.2 = (bf16[2048,256]{1,0:T(8,128)(2,1)S(1)}, bf16[2048,256]{1,0:T(8,128)(2,1)}, u32[]{:S(2)}) copy-start(bf16[2048,256]{1,0:T(8,128)(2,1)} %param.10) | copy-start | bytes 3145732
  6.5 66.6 %reduce-scatter.2.cloned.1.call-start = ((), (), s32[]{:S(2)}) async-start(), calls=%async_computation.1 | async-start | bytes 655360 | tf_op jit(solution)/shard_map/reduce_scatter | solution.py:83
  16.4 0.7 copy-start.5
  17.1 1.2 %copy-start.3 = (bf16[2048,256]{1,0:T(8,128)(2,1)S(1)}, bf16[2048,256]{1,0:T(8,128)(2,1)}, u32[]{:S(2)}) copy-start(bf16[2048,256]{1,0:T(8,128)(2,1)} %param.11) | copy-start | bytes 3145732
  18.3 1.2 %copy-start.4 = (bf16[2048,256]{1,0:T(8,128)(2,1)S(1)}, bf16[2048,256]{1,0:T(8,128)(2,1)}, u32[]{:S(2)}) copy-start(bf16[2048,256]{1,0:T(8,128)(2,1)} %param.9) | copy-start | bytes 3145732
  50.8 22.4 %copy-start.1 = (bf16[128,512]{1,0:T(8,128)(2,1)S(1)}, bf16[128,512]{1,0:T(8,128)(2,1)}, u32[]{:S(2)}) copy-start(bf16[128,512]{1,0:T(8,128)(2,1)} %param.7) | copy-start | bytes 393220
Sparse Core Ops, SparseCore 0:
  50.9 22.2 reduce-scatter.1
where the time goes:
time: 81.9 us; the launch traced here: 81.6 us
  blocking collectives  37.6 us (46%)
  waiting for transfers between devices  22.4 us (27%)
  between operations  13.5 us (16%)
  other arithmetic  3.1 us (4%)
  matrix products  2.85 us (3%)
  local copies, waits for them, and re-layouts  2.25 us (3%)
    reduce_scatter x1, waiting for transfers between devices, per_device(): lax.psum_scatter(partial_sums.astype(jnp.bfloat16), 'mp', scatter_dimensi...  22.4 us
    all_gather x1, blocking collectives, per_device(): lax.all_gather(key_rows, 'seq', axis=0, tiled=True)  14.6 us
    all_gather x1, blocking collectives, per_device(): lax.all_gather(value_rows, 'seq', axis=0, tiled=True)  14.1 us
    all_gather x1, blocking collectives, per_device(): full_rows = lax.all_gather(node_vectors, 'mp', axis=1, tiled=True)  8.84 us
    unnamed x12, local copies, waits for them, and re-layouts  2.11 us
  transfers between devices with their start and end apart: 1, of which 1 were waited for; matrix products, arithmetic and copies ran while one was open for 0% of the time, Pallas kernels for 0%

commit v1 on v0

--- a/solution.py
+++ b/solution.py
@@ -3,6 +3,18 @@
 import jax.numpy as jnp
 from jax import lax
 from jax.sharding import PartitionSpec as P
+
+
+def gather_by_bits(array, axis, dim):
+    ways, here = (lax.axis_size(axis), lax.axis_index(axis))
+    grown, reach = (array, 1)
+    while reach < ways:
+        theirs = lax.ppermute(grown, axis, [(d, d ^ reach) for d in range(ways)])
+        mine_first = jnp.concatenate([grown, theirs], axis=dim)
+        theirs_first = jnp.concatenate([theirs, grown], axis=dim)
+        grown = jnp.where(here & reach == 0, mine_first, theirs_first)
+        reach = 2 * reach
+    return grown
 
 
 def attend(state_in, blocks, query_heads, inverse_root_span, resident_groups, channel_span):
@@ -64,10 +76,7 @@
     )
     final = attend(
         initial,
-        (
-            lax.all_gather(key_rows, "seq", axis=0, tiled=True),
-            lax.all_gather(value_rows, "seq", axis=0, tiled=True),
-        ),
+        (gather_by_bits(key_rows, "seq", 0), lax.all_gather(value_rows, "seq", axis=0, tiled=True)),
         query_heads,
         inverse_root_span,
         resident_groups,

time: 81.9 us -> 74 us (0.904)
  blocking collectives: 37.6 us -> 23 us
  waiting for transfers between devices: 22.4 us -> 27.2 us
  starting transfers between devices: 0.01 us -> 2.36 us
  matrix products: 2.85 us -> 4.17 us
  local copies, waits for them, and re-layouts: 2.25 us -> 1.21 us
    all_gather x1 -> x0, blocking collectives: 14.6 us -> none  [per_device(): lax.all_gather(key_rows, 'seq', axis=0, tiled=True)]
    ppermute x0 -> x2, waiting for transfers between devices: none -> 6.54 us  [gather_by_bits(): theirs = lax.ppermute(grown, axis, [(d, d ^ reach) for d in range(ways)])]
    ppermute x0 -> x2, starting transfers between devices: none -> 2.36 us  [gather_by_bits(): theirs = lax.ppermute(grown, axis, [(d, d ^ reach) for d in range(ways)])]
    reduce_scatter x1, waiting for transfers between devices: 22.4 us -> 20.7 us  [per_device(): lax.psum_scatter(partial_sums.astype(jnp.bfloat16), 'mp', scatter_dimensi...]
    dot_general x1, matrix products: 0.36 us -> 1.67 us  [per_device(): jnp.dot(normed, content_matrix, preferred_element_type=jnp.float32)]
    unnamed x12, local copies, waits for them, and re-layouts: 2.11 us -> 1.05 us
  transfers between devices with their start and end apart: 1 -> 3, of which waited for: 1 -> 2; matrix products, arithmetic and copies ran while one was open for 0% -> 3% of each run, Pallas kernels for 0% -> 0%
where the time goes in v1:
time: 74 us; the launch traced here: 73.8 us
  waiting for transfers between devices  27.2 us (37%)
  blocking collectives  23 us (31%)
  between operations  13.5 us (18%)
  matrix products  4.17 us (6%)
  other arithmetic  2.37 us (3%)
  starting transfers between devices  2.36 us (3%)
  local copies, waits for them, and re-layouts  1.21 us (2%)
    reduce_scatter x1, waiting for transfers between devices, per_device(): lax.psum_scatter(partial_sums.astype(jnp.bfloat16), 'mp', scatter_dimensi...  20.7 us
    all_gather x1, blocking collectives, per_device(): lax.all_gather(value_rows, 'seq', axis=0, tiled=True)  14 us
    all_gather x1, blocking collectives, per_device(): full_rows = lax.all_gather(node_vectors, 'mp', axis=1, tiled=True)  8.97 us
    ppermute x2, waiting for transfers between devices, gather_by_bits(): theirs = lax.ppermute(grown, axis, [(d, d ^ reach) for d in range(ways)])  6.54 us
    ppermute x2, starting transfers between devices, gather_by_bits(): theirs = lax.ppermute(grown, axis, [(d, d ^ reach) for d in range(ways)])  2.36 us
    dot_general x1, matrix products, per_device(): jnp.dot(normed, content_matrix, preferred_element_type=jnp.float32)  1.67 us
    convert_element_type x1, other arithmetic, per_device(): return (node_vectors.astype(jnp.float32) + summed).astype(jnp.bfloat16)  1.59 us
  transfers between devices with their start and end apart: 3, of which 2 were waited for; matrix products, arithmetic and copies ran while one was open for 3% of the time, Pallas kernels for 0%

profile of v1, /device:TPU:0, one launch (start us, length us, event | category | flops | bytes accessed | tf_op | source)
XLA Modules:
  0.0 73.8 jit_solution(7276348698729742428)
XLA Ops:
  6.5 0.0 copy-start
  6.5 0.0 copy-start.2
  6.5 0.0 reduce-scatter.2.cloned.1.call-start
  6.5 9.0 %all_gather.6 = bf16[128,2048]{1,0:T(8,128)(2,1)S(1)} all-gather(bf16[128,512]{1,0:T(8,128)(2,1)} %param.7), channel_id=1, replica_groups=mesh['groups'=2,'seq'=4,'mp'=4] {'mp'}, dimensions={1}, use_global_device_ids=true | all-gather | bytes 655360 | tf_op jit(solution)/shard_map/all_gather | solution.py:53
  15.5 0.2 convert_reduce_fusion
  15.7 0.0 copy-start.4
  15.7 0.3 fusion.6
  16.0 0.0 copy-done.2
  16.0 0.4 copy-done.4
  16.4 0.4 convolution_convert_fusion.2
  16.7 1.6 %collective-permute-start = (bf16[128,256]{1,0:T(8,128)(2,1)S(1)}, bf16[128,256]{1,0:T(8,128)(2,1)S(1)}, u32[]{:S(2)}, u32[]{:S(2)}) collective-permute-start(bf16[128,256]{1,0:T(8,128)(2,1)S(1)} %convolution_convert_fusion.2), channel_id=1, source_target_pairs={{0,4},{4,0},{8,12},{12,8},{1,5},{5,1},{9,13},{13,9},{2,6},{6,2},{1... | collective-permute-start | bytes 196616 | tf_op jit(solution)/shard_map/ppermute | solution.py:12
  18.4 0.0 copy-start.5
  18.4 0.6 copy-done.5
  19.1 0.0 copy-start.3
  19.1 1.7 %convolution_convert_fusion.1 = bf16[128,256]{1,0:T(8,128)(2,1)S(1)} fusion(bf16[2048,256]{1,0:T(8,128)(2,1)} %param.11, bf16[128,2048]{1,0:T(8,128)(2,1)S(1)} %all_gather.6, f32[2048]{0:T(1024)S(1)} %copy-done.4, f32[128]{0:T(128)S(1)} %add_rsqrt_fusion, f32[128]{0:T(128)S(1)} %broadcast_multiply_fusion.1), kind=kOutput, calls=%fused_computation.10 | convolution fusion | flops 135561216 | bytes 1647616 | tf_op jit(solution)/shard_map/dot_general | solution.py:63
  20.7 0.0 copy-done.3
  20.8 0.4 fusion.5
  21.1 14.0 %all_gather.7 = bf16[512,256]{1,0:T(8,128)(2,1)S(1)} all-gather(bf16[128,256]{1,0:T(8,128)(2,1)S(1)} %convolution_convert_fusion.1), channel_id=1, replica_groups=mesh['groups'=2,'seq'=4,'mp'=4] {'seq'}, dimensions={0}, use_global_device_ids=true | all-gather | bytes 327680 | tf_op jit(solution)/shard_map/all_gather | solution.py:79
  35.1 0.1 copy.16
  35.3 0.0 collective-permute-done
  35.3 0.7 collective-permute-start.1
  36.1 6.5 %collective-permute-done.1 = bf16[256,256]{1,0:T(8,128)(2,1)S(1)} collective-permute-done((bf16[256,256]{1,0:T(8,128)(2,1)S(1)}, bf16[256,256]{1,0:T(8,128)(2,1)S(1)}, u32[]{:S(2)}, u32[]{:S(2)}) %collective-permute-start.1) | collective-permute-done | bytes 131104 | tf_op jit(solution)/shard_map/ppermute | solution.py:12
  42.6 0.3 fusion.25
  43.0 0.2 fusion.9
  43.2 0.3 fusion.4
  43.5 0.0 copy-done
  43.6 1.1 %convolution_convert_fusion = bf16[128,2048]{1,0:T(8,128)(2,1)} fusion(bf16[128,256]{0,1:T(8,128)(2,1)S(1)} %bitcast.45, bf16[256,2048]{1,0:T(8,128)(2,1)S(1)} %copy-done), kind=kOutput, calls=%fused_computation | convolution fusion | flops 134479872 | bytes 1638400 | tf_op jit(solution)/shard_map/dot_general | solution.py:91
  44.7 0.0 copy-start.1
  44.7 0.0 reduce-scatter.2.cloned.1.call-update
  44.7 20.7 %reduce-scatter.2.cloned.1.call-done = bf16[128,512]{1,0:T(8,128)(2,1)} async-done(((bf16[128,2048]{1,0:T(8,128)(2,1)}), bf16[128,512]{1,0:T(8,128)(2,1)}) %reduce-scatter.2.cloned.1.call-update) | async-done | bytes 131088 | tf_op jit(solution)/shard_map/reduce_scatter | solution.py:92
  65.4 0.0 copy-done.1
  65.4 1.6 %add_convert_fusion = bf16[128,512]{1,0:T(8,128)(2,1)} fusion(bf16[128,512]{1,0:T(8,128)(2,1)} %reduce-scatter.2.cloned.1.call-done, bf16[128,512]{1,0:T(8,128)(2,1)S(1)} %copy-done.1), kind=kLoop, calls=%fused_computation.26 | loop fusion | flops 262144 | bytes 393216 | tf_op jit(solution)/shard_map/convert_element_type | solution.py:95
  (10 shorter events, 0.1 us)
Async XLA Ops:
  6.5 37.0 %copy-start = (bf16[256,2048]{1,0:T(8,128)(2,1)S(1)}, bf16[256,2048]{1,0:T(8,128)(2,1)}, u32[]{:S(2)}) copy-start(bf16[256,2048]{1,0:T(8,128)(2,1)} %param.13) | copy-start | bytes 3145732
  6.5 9.4 %copy-start.2 = (bf16[2048,256]{1,0:T(8,128)(2,1)S(1)}, bf16[2048,256]{1,0:T(8,128)(2,1)}, u32[]{:S(2)}) copy-start(bf16[2048,256]{1,0:T(8,128)(2,1)} %param.10) | copy-start | bytes 3145732
  6.5 58.8 %reduce-scatter.2.cloned.1.call-start = ((), (), s32[]{:S(2)}) async-start(), calls=%async_computation.1 | async-start | bytes 655360 | tf_op jit(solution)/shard_map/reduce_scatter | solution.py:92
  15.7 0.7 copy-start.4
  16.7 18.5 %collective-permute-start = (bf16[128,256]{1,0:T(8,128)(2,1)S(1)}, bf16[128,256]{1,0:T(8,128)(2,1)S(1)}, u32[]{:S(2)}, u32[]{:S(2)}) collective-permute-start(bf16[128,256]{1,0:T(8,128)(2,1)S(1)} %convolution_convert_fusion.2), channel_id=1, source_target_pairs={{0,4},{4,0},{8,12},{12,8},{1,5},{5,1},{9,13},{13,9},{2,6},{6,2},{1... | collective-permute-start | bytes 196616 | tf_op jit(solution)/shard_map/ppermute | solution.py:12
  18.4 0.7 copy-start.5
  19.1 1.7 %copy-start.3 = (bf16[2048,256]{1,0:T(8,128)(2,1)S(1)}, bf16[2048,256]{1,0:T(8,128)(2,1)}, u32[]{:S(2)}) copy-start(bf16[2048,256]{1,0:T(8,128)(2,1)} %param.9) | copy-start | bytes 3145732
  35.3 7.3 %collective-permute-start.1 = (bf16[256,256]{1,0:T(8,128)(2,1)S(1)}, bf16[256,256]{1,0:T(8,128)(2,1)S(1)}, u32[]{:S(2)}, u32[]{:S(2)}) collective-permute-start(bf16[256,256]{1,0:T(8,128)(2,1)S(1)} %maximum_select_fusion.3), channel_id=1, source_target_pairs={{0,8},{4,12},{8,0},{12,4},{1,9},{5,13},{9,1},{13,5},{2,10},{6,14},... | collective-permute-start | bytes 393224 | tf_op jit(solution)/shard_map/ppermute | solution.py:12
  44.7 20.7 %copy-start.1 = (bf16[128,512]{1,0:T(8,128)(2,1)S(1)}, bf16[128,512]{1,0:T(8,128)(2,1)}, u32[]{:S(2)}) copy-start(bf16[128,512]{1,0:T(8,128)(2,1)} %param.7) | copy-start | bytes 393220
Sparse Core Ops, SparseCore 0:
  44.8 20.4 reduce-scatter.1
